TPU v7x, 32 devices: a whole 2x2x4 slice. The times are simulated.
32 devices in a mesh: dp: 8 (over z, x), seq: 4 (over y, core).
Axes of the slice: x: 2, y: 2, z: 4, core: 2. Of those that a mesh axis runs over, the one named last changes fastest.
Arguments:
- tokens: bfloat16 [16384, 1024], P(('dp', 'seq')), may hold values from -6 to 6
- time_embed: bfloat16 [32, 1024], P(('dp', 'seq')), may hold values from -6 to 6
- lengths: int32 [32], P('dp'), may hold values from 0 to 475, as said below
- cotangent: bfloat16 [16384, 1024], P(('dp', 'seq')), may hold values from -6 to 6
- w_query: bfloat16 [1024, 1024], P('seq'), may hold values from -0.1875 to 0.1875
- w_key: bfloat16 [1024, 1024], P('seq'), may hold values from -0.1875 to 0.1875
- w_value: bfloat16 [1024, 1024], P('seq'), may hold values from -0.1875 to 0.1875
- w_out: bfloat16 [1024, 1024], P('seq'), may hold values from -0.75 to 0.75
- w_time: bfloat16 [1024, 1024], P('seq'), may hold values from -0.1875 to 0.1875
- w_in: bfloat16 [4096, 1024], P('seq'), may hold values from -0.1875 to 0.1875
- w_down: bfloat16 [4096, 1024], P('seq'), may hold values from -0.09375 to 0.09375
- b_query: bfloat16 [1024], replicated, may hold values from -3 to 3
- b_value: bfloat16 [1024], replicated, may hold values from -3 to 3
- b_out: bfloat16 [1024], replicated, may hold values from -3 to 3
- b_time: bfloat16 [1024], replicated, may hold values from -3 to 3
- b_in: bfloat16 [4096], replicated, may hold values from -3 to 3
- b_down: bfloat16 [1024], replicated, may hold values from -2 to 2
- gain_one: bfloat16 [1024], replicated, may hold values from 0.25 to 1.75
- shift_one: bfloat16 [1024], replicated, may hold values from -2 to 2
- gain_two: bfloat16 [1024], replicated, may hold values from 0.25 to 1.75
- shift_two: bfloat16 [1024], replicated, may hold values from -2 to 2
Outputs:
- layer_out: bfloat16 [16384, 1024], P(('dp', 'seq'))
- grad_tokens: bfloat16 [16384, 1024], P(('dp', 'seq'))
- grad_w_query: float32 [1024, 1024], P('seq')
- grad_w_key: float32 [1024, 1024], P('seq')
- grad_w_value: float32 [1024, 1024], P('seq')
- grad_w_out: float32 [1024, 1024], P('seq')
- grad_w_time: float32 [1024, 1024], P('seq')
- grad_w_in: float32 [4096, 1024], P('seq')
- grad_w_down: float32 [4096, 1024], P('seq')
- grad_b_query: float32 [1024], replicated
- grad_b_value: float32 [1024], replicated
- grad_b_out: float32 [1024], replicated
- grad_b_time: float32 [1024], replicated
- grad_b_in: float32 [4096], replicated
- grad_b_down: float32 [1024], replicated
- grad_gain_one: float32 [1024], replicated
- grad_shift_one: float32 [1024], replicated
- grad_gain_two: float32 [1024], replicated
- grad_shift_two: float32 [1024], replicated
Inputs may be any that keep to these rules, and one draw needn't show every extreme that they name: Item i's valid slots are its first lengths[i] + 25; every draw has an item of length 475 and one of length 0.
All inputs are finite; a program needn't handle non-finite values.
Results may differ from a plain program's by a relative error of at most 0.02.
Values may be sent and summed in bfloat16 or wider, within the bound.
A program may use at most 256 MiB of HBM per device.

v0:
```python
import jax
import jax.numpy as jnp
from jax import lax
from jax.sharding import PartitionSpec as P

HEAD_DIM = 64
BLOCK = 25
norm_eps = 1e-05
neg_large = -1e30


def layer_norm(values, gain, shift):
    center = values - jnp.mean(values, axis=-1, keepdims=True)
    spread = lax.rsqrt(jnp.mean(center * center, axis=-1, keepdims=True) + norm_eps)
    return center * spread * gain + shift


def exact_gelu(values):
    return jax.nn.gelu(values, approximate=False)


def split_heads(rows):
    return rows.reshape(rows.shape[0], rows.shape[1] // HEAD_DIM, HEAD_DIM)


def item_scores(item_block, key_valid):
    queries = split_heads(item_block[:, 0])
    key_heads = split_heads(item_block[:, 1])
    value_heads = split_heads(item_block[:, 2])
    scores = jnp.einsum(
        "qhd,khd->hqk", queries, key_heads, preferred_element_type=jnp.float32
    ) * HEAD_DIM ** (-0.5)
    masked = jnp.where(key_valid[None, None, :], scores, neg_large)
    return (queries, key_heads, value_heads, masked)


def attend_forward(packed):
    item_block, key_valid = packed
    queries, key_heads, value_heads, masked = item_scores(item_block, key_valid)
    row_max = jnp.max(masked, axis=-1, keepdims=True)
    exp_scores = jnp.exp(masked - row_max)
    row_total = jnp.sum(exp_scores, axis=-1, keepdims=True)
    soft_weights = (exp_scores / row_total).astype(jnp.bfloat16)
    mixed_heads = jnp.einsum(
        "hqk,khd->qhd", soft_weights, value_heads, preferred_element_type=jnp.float32
    )
    log_total = row_max[:, :, 0] + jnp.log(row_total[:, :, 0])
    return (mixed_heads.reshape(item_block.shape[0], -1).astype(jnp.bfloat16), log_total)


def attend_backward(packed):
    item_block, key_valid, log_total, grad_block = packed
    queries, key_heads, value_heads, masked = item_scores(item_block, key_valid)
    soft_weights = jnp.exp(masked - log_total[:, :, None])
    grad_heads = split_heads(grad_block)
    grad_value = jnp.einsum(
        "hqk,qhd->khd",
        soft_weights.astype(jnp.bfloat16),
        grad_heads,
        preferred_element_type=jnp.float32,
    )
    grad_soft = jnp.einsum(
        "qhd,khd->hqk", grad_heads, value_heads, preferred_element_type=jnp.float32
    )
    grad_scores = soft_weights * (
        grad_soft - jnp.sum(soft_weights * grad_soft, axis=-1, keepdims=True)
    )
    scores_low = grad_scores.astype(jnp.bfloat16)
    score_scale = HEAD_DIM ** (-0.5)
    grad_query = (
        jnp.einsum("hqk,khd->qhd", scores_low, key_heads, preferred_element_type=jnp.float32)
        * score_scale
    )
    grad_key = (
        jnp.einsum("hqk,qhd->khd", scores_low, queries, preferred_element_type=jnp.float32)
        * score_scale
    )
    slot_count = item_block.shape[0]
    return jnp.stack(
        [
            grad_query.reshape(slot_count, -1),
            grad_key.reshape(slot_count, -1),
            grad_value.reshape(slot_count, -1),
        ],
        axis=1,
    ).astype(jnp.bfloat16)


def local(
    tokens,
    time_embed,
    lengths,
    cotangent,
    w_query,
    w_key,
    w_value,
    w_out,
    w_time,
    w_in,
    w_down,
    b_query,
    b_value,
    b_out,
    b_time,
    b_in,
    b_down,
    gain_one,
    shift_one,
    gain_two,
    shift_two,
):
    seq_rank = lax.axis_index("seq")
    item_count = time_embed.shape[0]
    token_count = tokens.shape[0]
    slot_count = token_count // item_count
    model_width = tokens.shape[1]
    full_query, full_key, full_value, full_out, full_time, full_in, full_down = (
        lax.all_gather(w_query, "seq", axis=0, tiled=True),
        lax.all_gather(w_key, "seq", axis=0, tiled=True),
        lax.all_gather(w_value, "seq", axis=0, tiled=True),
        lax.all_gather(w_out, "seq", axis=0, tiled=True),
        lax.all_gather(w_time, "seq", axis=0, tiled=True),
        lax.all_gather(w_in, "seq", axis=0, tiled=True),
        lax.all_gather(w_down, "seq", axis=0, tiled=True),
    )
    bias_query = b_query.astype(jnp.float32)
    bias_value = b_value.astype(jnp.float32)
    bias_out = b_out.astype(jnp.float32)
    bias_time = b_time.astype(jnp.float32)
    bias_in = b_in.astype(jnp.float32)
    bias_down = b_down.astype(jnp.float32)
    gain_first = gain_one.astype(jnp.float32)
    shift_first = shift_one.astype(jnp.float32)
    gain_last = gain_two.astype(jnp.float32)
    shift_last = shift_two.astype(jnp.float32)
    slot_index = lax.broadcasted_iota(jnp.int32, (lengths.shape[0], slot_count), 1)
    group_valid = slot_index < lengths[:, None] + BLOCK
    own_valid = lax.dynamic_slice_in_dim(group_valid, seq_rank * item_count, item_count, 0)
    row_keep = own_valid.reshape(token_count, 1).astype(jnp.float32)
    time_proj = jnp.dot(time_embed, full_time, preferred_element_type=jnp.float32) + bias_time
    resid = (tokens.reshape(item_count, slot_count, model_width) + time_proj[:, None, :]).reshape(
        token_count, model_width
    )
    resid_low = resid.astype(jnp.bfloat16)
    query_rows = (
        jnp.dot(resid_low, full_query, preferred_element_type=jnp.float32) + bias_query
    ).astype(jnp.bfloat16)
    key_rows = jnp.dot(resid_low, full_key, preferred_element_type=jnp.float32).astype(jnp.bfloat16)
    value_rows = (
        jnp.dot(resid_low, full_value, preferred_element_type=jnp.float32) + bias_value
    ).astype(jnp.bfloat16)
    stacked = jnp.stack([query_rows, key_rows, value_rows], axis=1).reshape(
        item_count, slot_count, 3, model_width
    )
    head_side = lax.all_to_all(stacked, "seq", split_axis=3, concat_axis=0, tiled=True)
    mixed_heads, log_totals = lax.map(attend_forward, (head_side, group_valid))
    mixed_rows = lax.all_to_all(
        mixed_heads, "seq", split_axis=0, concat_axis=2, tiled=True
    ).reshape(token_count, model_width)
    attn_out = jnp.dot(mixed_rows, full_out, preferred_element_type=jnp.float32) + bias_out
    first_norm, first_pull = jax.vjp(layer_norm, resid + attn_out, gain_first, shift_first)
    first_low = first_norm.astype(jnp.bfloat16)
    hidden_pre = (
        jnp.einsum("td,fd->tf", first_low, full_in, preferred_element_type=jnp.float32) + bias_in
    )
    hidden, gelu_pull = jax.vjp(exact_gelu, hidden_pre)
    hidden_low = hidden.astype(jnp.bfloat16)
    ffn_out = jnp.dot(hidden_low, full_down, preferred_element_type=jnp.float32) + bias_down
    second_norm, second_pull = jax.vjp(layer_norm, first_norm + ffn_out, gain_last, shift_last)
    layer_out = (second_norm * row_keep).astype(jnp.bfloat16)
    back_query, back_key, back_value, back_out, back_in, back_down = (
        lax.all_gather(w_query, "seq", axis=0, tiled=True),
        lax.all_gather(w_key, "seq", axis=0, tiled=True),
        lax.all_gather(w_value, "seq", axis=0, tiled=True),
        lax.all_gather(w_out, "seq", axis=0, tiled=True),
        lax.all_gather(w_in, "seq", axis=0, tiled=True),
        lax.all_gather(w_down, "seq", axis=0, tiled=True),
    )
    grad_second_in, grad_gain_two, grad_shift_two = second_pull(
        cotangent.astype(jnp.float32) * row_keep
    )
    grad_ffn = grad_second_in.astype(jnp.bfloat16)
    grad_hidden = jnp.einsum("td,fd->tf", grad_ffn, back_down, preferred_element_type=jnp.float32)
    grad_pre = gelu_pull(grad_hidden)[0].astype(jnp.bfloat16)
    grad_first = grad_second_in + jnp.dot(grad_pre, back_in, preferred_element_type=jnp.float32)
    grad_first_in, grad_gain_one, grad_shift_one = first_pull(grad_first)
    grad_attn = grad_first_in.astype(jnp.bfloat16)
    grad_mixed = jnp.einsum(
        "td,ed->te", grad_attn, back_out, preferred_element_type=jnp.float32
    ).astype(jnp.bfloat16)
    grad_heads = lax.all_to_all(
        grad_mixed.reshape(item_count, slot_count, model_width),
        "seq",
        split_axis=2,
        concat_axis=0,
        tiled=True,
    )
    grad_stack = lax.map(attend_backward, (head_side, group_valid, log_totals, grad_heads))
    grad_qkv = lax.all_to_all(grad_stack, "seq", split_axis=0, concat_axis=3, tiled=True).reshape(
        token_count, 3, model_width
    )
    grad_query_rows = grad_qkv[:, 0]
    grad_key_rows = grad_qkv[:, 1]
    grad_value_rows = grad_qkv[:, 2]
    grad_resid = grad_first_in + jnp.einsum(
        "te,de->td", grad_query_rows, back_query, preferred_element_type=jnp.float32
    )
    grad_resid = grad_resid + jnp.einsum(
        "te,de->td", grad_key_rows, back_key, preferred_element_type=jnp.float32
    )
    grad_resid = grad_resid + jnp.einsum(
        "te,de->td", grad_value_rows, back_value, preferred_element_type=jnp.float32
    )
    grad_tokens = grad_resid.astype(jnp.bfloat16)
    grad_time = jnp.sum(grad_resid.reshape(item_count, slot_count, model_width), axis=1).astype(
        jnp.bfloat16
    )
    term_in = jnp.einsum("tf,td->fd", grad_pre, first_low, preferred_element_type=jnp.float32)
    term_down = jnp.einsum("tf,td->fd", hidden_low, grad_ffn, preferred_element_type=jnp.float32)
    ffn_share = lax.psum_scatter(
        jnp.concatenate([term_in, term_down], axis=1).astype(jnp.bfloat16),
        "seq",
        scatter_dimension=0,
        tiled=True,
    ).astype(jnp.float32)
    share_in = ffn_share[:, :model_width]
    share_down = ffn_share[:, model_width:]
    grad_qkv_flat = grad_qkv.reshape(token_count, 3 * model_width)
    term_qkv = jnp.einsum("tr,te->re", resid_low, grad_qkv_flat, preferred_element_type=jnp.float32)
    term_out = jnp.einsum("tr,te->re", mixed_rows, grad_attn, preferred_element_type=jnp.float32)
    term_time = jnp.einsum("tr,te->re", time_embed, grad_time, preferred_element_type=jnp.float32)
    attn_share = lax.psum_scatter(
        jnp.concatenate([term_qkv, term_out, term_time], axis=1).astype(jnp.bfloat16),
        "seq",
        scatter_dimension=0,
        tiled=True,
    ).astype(jnp.float32)
    sum_in, sum_down, sum_attn = lax.psum((share_in, share_down, attn_share), "dp")
    (
        grad_b_query,
        grad_b_value,
        grad_b_out,
        grad_b_time,
        grad_b_in,
        grad_b_down,
        sum_gain_one,
        sum_shift_one,
        sum_gain_two,
        sum_shift_two,
    ) = lax.psum(
        (
            jnp.sum(grad_query_rows, axis=0, dtype=jnp.float32),
            jnp.sum(grad_value_rows, axis=0, dtype=jnp.float32),
            jnp.sum(grad_attn, axis=0, dtype=jnp.float32),
            jnp.sum(grad_time, axis=0, dtype=jnp.float32),
            jnp.sum(grad_pre, axis=0, dtype=jnp.float32),
            jnp.sum(grad_ffn, axis=0, dtype=jnp.float32),
            grad_gain_one,
            grad_shift_one,
            grad_gain_two,
            grad_shift_two,
        ),
        ("dp", "seq"),
    )
    return (
        layer_out,
        grad_tokens,
        sum_attn[:, :model_width],
        sum_attn[:, model_width : 2 * model_width],
        sum_attn[:, 2 * model_width : 3 * model_width],
        sum_attn[:, 3 * model_width : 4 * model_width],
        sum_attn[:, 4 * model_width :],
        sum_in,
        sum_down,
        grad_b_query,
        grad_b_value,
        grad_b_out,
        grad_b_time,
        grad_b_in,
        grad_b_down,
        sum_gain_one,
        sum_shift_one,
        sum_gain_two,
        sum_shift_two,
    )


def solution(mesh):
    in_specs = (
        P(("dp", "seq"), None),
        P(("dp", "seq"), None),
        P("dp"),
        P(("dp", "seq"), None),
        P("seq", None),
        P("seq", None),
        P("seq", None),
        P("seq", None),
        P("seq", None),
        P("seq", None),
        P("seq", None),
        P(),
        P(),
        P(),
        P(),
        P(),
        P(),
        P(),
        P(),
        P(),
        P(),
    )
    out_specs = (
        P(("dp", "seq"), None),
        P(("dp", "seq"), None),
        P("seq", None),
        P("seq", None),
        P("seq", None),
        P("seq", None),
        P("seq", None),
        P("seq", None),
        P("seq", None),
        P(),
        P(),
        P(),
        P(),
        P(),
        P(),
        P(),
        P(),
        P(),
        P(),
    )
    return jax.shard_map(local, mesh=mesh, in_specs=in_specs, out_specs=out_specs, check_vma=False)
```

profile of v0, /device:TPU:0, one launch (start us, length us, event | category | flops | bytes accessed | tf_op | source)
XLA Modules:
  0.0 1024.9 jit_solution(11175937221474394372)
XLA Ops:
  11.2 23.7 %all-gather.8.cloned.1.call-done = bf16[1024,1024]{1,0:T(8,128)(2,1)} async-done(((bf16[256,1024]{1,0:T(8,128)(2,1)}), bf16[1024,1024]{1,0:T(8,128)(2,1)}) %all-gather.8.cloned.1.call-update) | async-done | bytes 2097168 | tf_op jit(solution)/shard_map/all_gather | solution.py:122
  36.9 22.2 %all-gather.12.cloned.1.call-done = bf16[1024,1024]{1,0:T(8,128)(2,1)} async-done(((bf16[256,1024]{1,0:T(8,128)(2,1)}), bf16[1024,1024]{1,0:T(8,128)(2,1)}) %all-gather.12.cloned.1.call-update) | async-done | bytes 2097168 | tf_op jit(solution)/shard_map/all_gather | solution.py:119
  62.9 20.3 %all-gather.10.cloned.1.call-done = bf16[1024,1024]{1,0:T(8,128)(2,1)} async-done(((bf16[256,1024]{1,0:T(8,128)(2,1)}), bf16[1024,1024]{1,0:T(8,128)(2,1)}) %all-gather.10.cloned.1.call-update) | async-done | bytes 2097168 | tf_op jit(solution)/shard_map/all_gather | solution.py:118
  87.1 20.2 %all-gather.14.cloned.1.call-done = bf16[1024,1024]{1,0:T(8,128)(2,1)} async-done(((bf16[256,1024]{1,0:T(8,128)(2,1)}), bf16[1024,1024]{1,0:T(8,128)(2,1)}) %all-gather.14.cloned.1.call-update) | async-done | bytes 2097168 | tf_op jit(solution)/shard_map/all_gather | solution.py:120
  110.6 5.7 copy.80
  116.3 5.1 all-to-all-start
  122.3 77.5 %all-to-all-done = bf16[1,512,3,1024]{1,2,0,3:T(4,128)(2,1)} async-done(((bf16[1,512,3,1024]{1,2,0,3:T(4,128)(2,1)}), bf16[1,512,3,1024]{1,2,0,3:T(4,128)(2,1)}, u32[]{:S(2)}, u32[]{:S(2)}) %all-to-all-start) | async-done | bytes 3145760 | tf_op jit(solution)/shard_map/all_to_all | solution.py:155
  202.9 16.3 %while.22 = (s32[]{:T(128)}, bf16[4,512,256]{1,2,0:T(8,128)(2,1)}, f32[4,4,512]{2,1,0:T(4,128)S(1)}, bf16[4,512,3,256]{1,3,2,0:T(8,128)(2,1)S(1)}, pred[4,512]{1,0:T(4,128)(4,1)S(1)}, /*index=5*/s32[]{:T(128)}) while((s32[]{:T(128)}, bf16[4,512,256]{1,2,0:T(8,128)(2,1)}, f32[4,4,512]{2,1,0:T(4,128)S(1)}, ...), condition=%wide.region_3.4_spmd, body=%wide.region_0.3_spmd.sunk | while | flops 281147392 | bytes 17370192 | solution.py:156
  223.7 18.0 %all-to-all-done.1 = bf16[4,512,256]{1,2,0:T(8,128)(2,1)} async-done(((bf16[4,512,256]{1,2,0:T(8,128)(2,1)}), bf16[4,512,256]{1,2,0:T(8,128)(2,1)}, u32[]{:S(2)}, u32[]{:S(2)}) %all-to-all-start.1) | async-done | bytes 1048608 | tf_op jit(solution)/shard_map/all_to_all | solution.py:157
  247.0 27.2 %multiply_convert_fusion.1 = (bf16[512,4096]{1,0:T(8,128)(2,1)}, f32[512,4096]{1,0:T(8,128)}, f32[512,4096]{1,0:T(8,128)}) fusion(f32[4096]{0:T(1024)S(1)} %convert_element_type.170, bf16[4096,1024]{1,0:T(8,128)(2,1)} %all-gather.18.cloned.1.call-done, f32[512,1024]{1,0:T(8,128)} %copy-done, f32[1024]{0:T(1024)S(1)} %convert_element_type.168, ...), kind=kOutput, calls=%fused_computation.37 | convolution fusion | flops 4436000768 | bytes 31485952 | tf_op jit(solution)/shard_map/td,fd->tf/dot_general | solution.py:164
  274.2 10.3 %all-gather.20.cloned.1.call-done = bf16[4096,1024]{1,0:T(8,128)(2,1)} async-done(((bf16[1024,1024]{1,0:T(8,128)(2,1)}), bf16[4096,1024]{1,0:T(8,128)(2,1)}) %all-gather.20.cloned.1.call-update) | async-done | bytes 8388624 | tf_op jit(solution)/shard_map/all_gather | solution.py:124
  284.5 10.0 fusion.59
  300.6 7.1 convolution_convert_fusion
  307.7 13.5 %convert_reduce_fusion = (f32[4096]{0:T(1024)S(1)}, bf16[512,4096]{1,0:T(8,128)(2,1)S(1)}) fusion(f32[512,4096]{1,0:T(8,128)} %get-tuple-element.209, f32[512,4096]{1,0:T(8,128)} %get-tuple-element.234, f32[4096]{0:T(1024)S(1)} %convert_element_type.170, bf16[512,1024]{1,0:T(8,128)(2,1)S(1)} %get-tuple-element.199, ...), kind=kOutput, calls=%fused_computation.35 | convolution fusion | flops 4330614784 | bytes 30441472 | tf_op jit(solution)/shard_map/td,fd->tf/dot_general | solution.py:183
  321.3 7.0 convolution_convert_fusion.1
  328.3 13.9 %pad_maximum_fusion = bf16[4096,2048]{0,1:T(8,128)(2,1)} fusion(bf16[4096,1024]{0,1:T(8,128)(2,1)} %convolution_convert_fusion, bf16[4096,1024]{0,1:T(8,128)(2,1)} %convolution_convert_fusion.1), kind=kLoop, calls=%fused_computation.31 | loop fusion | flops 33554432 | bytes 33554432 | tf_op jit(solution)/shard_map/concatenate | solution.py:221
  342.2 11.4 %multiply_reduce_fusion.2 = (f32[1024]{0:T(1024)S(1)}, f32[512]{0:T(512)S(1)}, f32[1024]{0:T(1024)S(1)}, f32[512,1024]{1,0:T(8,128)S(1)}) fusion(f32[512,1024]{1,0:T(8,128)} %copy-done, f32[512]{0:T(512)S(1)} %fusion.42, f32[512]{0:T(512)S(1)} %broadcast_multiply_fusion.1, f32[1024]{0:T(1024)S(1)} %convert_element_type.167, ...), kind=kOutput, calls=%fused_computation.61 | convolution fusion | flops 4300207616 | bytes 18894848 | tf_op jit(solution)/shard_map/dot_general | solution.py:185
  359.2 6.2 copy.82
  365.9 9.0 reduce.7
  378.8 4.3 all-to-all-start.2
  383.1 26.1 %all-to-all-done.2 = bf16[4,2,65536]{2,1,0:T(2,128)(2,1)} async-done(((bf16[4,2,65536]{2,1,0:T(2,128)(2,1)}), bf16[4,2,65536]{2,1,0:T(2,128)(2,1)}, u32[]{:S(2)}, u32[]{:S(2)}) %all-to-all-start.2) | async-done | bytes 1048608 | tf_op jit(solution)/shard_map/all_to_all | solution.py:191
  416.1 35.0 %while.23 = (s32[]{:T(128)}, bf16[4,512,3,256]{1,3,2,0:T(8,128)(2,1)}, bf16[4,512,3,256]{1,3,2,0:T(8,128)(2,1)S(1)}, pred[4,512]{1,0:T(4,128)(4,1)S(1)}, f32[4,4...) while((s32[]{:T(128)}, bf16[4,512,3,256]{1,3,2,0:T(8,128)(2,1)}, ...), condition=%wide.region_14.15_spmd, body=%wide.region_12.14_spmd.sunk | while | flops 689829888 | bytes 39382108 | solution.py:198
  459.2 51.5 %all-to-all-done.3 = bf16[4,512,3,256]{1,3,2,0:T(8,128)(2,1)S(1)} async-done(((bf16[4,512,3,256]{1,3,2,0:T(8,128)(2,1)}), bf16[4,512,3,256]{1,3,2,0:T(8,128)(2,1)S(1)}, u32[]{:S(2)}, u32[]{:S(2)}) %all-to-all-start.3) | async-done | bytes 3145760 | tf_op jit(solution)/shard_map/all_to_all | solution.py:199
  524.0 9.9 pad_maximum_fusion.1
  534.0 6.8 fusion.55
  548.6 41.3 %all-reduce = (f32[1024]{0:T(1024)}, f32[1024]{0:T(1024)}, f32[1024]{0:T(1024)}, f32[1024]{0:T(1024)}, f32[4096]{0:T(1024)}, /*index=5*/f32[1024]{0:T(1024)}, f3...) all-reduce(f32[1024]{0:T(1024)S(1)} %get-tuple-element.240, ...), channel_id=1, replica_groups=mesh['dp'=8,'seq'=4] {'dp','seq'}, use_global_device_ids=true, to_apply=%region_22.23 | all-reduce | flops 13312 | bytes 104448 | tf_op jit(solution)/shard_map/psum | solution.py:250
  589.9 29.4 %reduce-scatter.3.cloned.1.call-done = bf16[256,5120]{1,0:T(8,128)(2,1)} async-done(((bf16[1024,5120]{1,0:T(8,128)(2,1)}), bf16[256,5120]{1,0:T(8,128)(2,1)}) %reduce-scatter.3.cloned.1.call-update) | async-done | bytes 2621456 | tf_op jit(solution)/shard_map/reduce_scatter | solution.py:232
  619.3 267.7 %all-reduce.6 = f32[256,5120]{1,0:T(8,128)} all-reduce(bf16[256,5120]{1,0:T(8,128)(2,1)} %reduce-scatter.3.cloned.1.call-done), channel_id=1, replica_groups=mesh['dp'=8,'seq'=4] {'dp'}, use_global_device_ids=true, to_apply=%region_17.18 | all-reduce | flops 1310720 | bytes 7864320 | tf_op jit(solution)/shard_map/psum | solution.py:238
  887.0 5.0 fusion.54
  892.0 114.9 %all-reduce.5.cloned.1.call-done = (f32[1024,1024]{0,1:T(8,128)}, f32[1024,1024]{0,1:T(8,128)}) async-done(((f32[1024,1024]{0,1:T(8,128)}, f32[1024,1024]{0,1:T(8,128)}), (f32[1024,1024]{0,1:T(8,128)}, f32[1024,1024]{0,1:T(8,128)})) %all-reduce.5.cloned.1.call-update) | async-done | bytes 8388624 | tf_op jit(solution)/shard_map/psum | solution.py:238
  1006.9 5.3 copy.88
  1012.3 5.3 copy.89
  (242 shorter events, 133.4 us)
Async XLA Ops:
  7.2 27.7 %copy-start.22 = (bf16[1,1024]{1,0:T(2,128)(2,1)S(1)}, bf16[1,1024]{1,0:T(2,128)(2,1)}, u32[]{:S(2)}) copy-start(bf16[1,1024]{1,0:T(2,128)(2,1)} %param.26) | copy-start | bytes 6148
  7.2 29.7 %copy-start.27 = (bf16[1024]{0:T(1024)(128)(2,1)S(1)}, bf16[1024]{0:T(1024)(128)(2,1)}, u32[]{:S(2)}) copy-start(bf16[1024]{0:T(1024)(128)(2,1)} %param.39) | copy-start | bytes 6148
  7.2 51.9 %copy-start.12 = (bf16[512,1024]{1,0:T(8,128)(2,1)S(1)}, bf16[512,1024]{1,0:T(8,128)(2,1)}, u32[]{:S(2)}) copy-start(bf16[512,1024]{1,0:T(8,128)(2,1)} %param.25) | copy-start | bytes 3145732
  7.2 27.7 %all-gather.8.cloned.1.call-start = ((), (), s32[]{:S(2)}) async-start(), calls=%async_computation.6 | async-start | bytes 2621440 | tf_op jit(solution)/shard_map/all_gather | solution.py:122
  8.0 51.1 %all-gather.12.cloned.1.call-start = ((), (), s32[]{:S(2)}) async-start(), calls=%async_computation.8 | async-start | bytes 2621440 | tf_op jit(solution)/shard_map/all_gather | solution.py:119
  8.7 74.5 %all-gather.10.cloned.1.call-start = ((), (), s32[]{:S(2)}) async-start(), calls=%async_computation.7 | async-start | bytes 2621440 | tf_op jit(solution)/shard_map/all_gather | solution.py:118
  9.5 97.8 %all-gather.14.cloned.1.call-start = ((), (), s32[]{:S(2)}) async-start(), calls=%async_computation.9 | async-start | bytes 2621440 | tf_op jit(solution)/shard_map/all_gather | solution.py:120
  10.0 213.6 %all-gather.16.cloned.1.call-start = ((), (), s32[]{:S(2)}) async-start(), calls=%async_computation.10 | async-start | bytes 2621440 | tf_op jit(solution)/shard_map/all_gather | solution.py:121
  10.6 236.4 %all-gather.18.cloned.1.call-start = ((), (), s32[]{:S(2)}) async-start(), calls=%async_computation.11 | async-start | bytes 10485760 | tf_op jit(solution)/shard_map/all_gather | solution.py:123
  36.9 204.8 %copy-start.16 = (f32[1024]{0:T(1024)}, f32[1024]{0:T(1024)S(1)}, u32[]{:S(2)}) copy-start(f32[1024]{0:T(1024)S(1)} %convert_add_fusion.1) | copy-start | bytes 12292
  116.3 5.8 copy-start.37
  116.3 83.5 %all-to-all-start = ((bf16[1,512,3,1024]{1,2,0,3:T(4,128)(2,1)}), bf16[1,512,3,1024]{1,2,0,3:T(4,128)(2,1)}, u32[]{:S(2)}, u32[]{:S(2)}) async-start(bf16[1,512,3,1024]{1,2,0,3:T(4,128)(2,1)} %copy.80), calls=%async_computation | async-start | bytes 8388608 | tf_op jit(solution)/shard_map/all_to_all | solution.py:155
  121.4 163.1 %all-gather.20.cloned.1.call-start = ((), (), s32[]{:S(2)}) async-start(), calls=%async_computation.12 | async-start | bytes 10485760 | tf_op jit(solution)/shard_map/all_gather | solution.py:124
  202.8 20.7 %copy-start.28 = (bf16[1024]{0:T(1024)(128)(2,1)S(1)}, bf16[1024]{0:T(1024)(128)(2,1)}, u32[]{:S(2)}) copy-start(bf16[1024]{0:T(1024)(128)(2,1)} %param.38) | copy-start | bytes 6148
  202.8 20.7 %copy-start.29 = (bf16[1024]{0:T(1024)(128)(2,1)S(1)}, bf16[1024]{0:T(1024)(128)(2,1)}, u32[]{:S(2)}) copy-start(bf16[1024]{0:T(1024)(128)(2,1)} %param.42) | copy-start | bytes 6148
  202.8 20.7 %copy-start.30 = (bf16[1024]{0:T(1024)(128)(2,1)S(1)}, bf16[1024]{0:T(1024)(128)(2,1)}, u32[]{:S(2)}) copy-start(bf16[1024]{0:T(1024)(128)(2,1)} %param.43) | copy-start | bytes 6148
  202.8 20.7 %copy-start.24 = (bf16[4096]{0:T(1024)(128)(2,1)S(1)}, bf16[4096]{0:T(1024)(128)(2,1)}, u32[]{:S(2)}) copy-start(bf16[4096]{0:T(1024)(128)(2,1)} %param.40) | copy-start | bytes 24580
  202.8 20.7 %copy-start.31 = (bf16[1024]{0:T(1024)(128)(2,1)S(1)}, bf16[1024]{0:T(1024)(128)(2,1)}, u32[]{:S(2)}) copy-start(bf16[1024]{0:T(1024)(128)(2,1)} %param.41) | copy-start | bytes 6148
  202.9 20.7 %copy-start.32 = (bf16[1024]{0:T(1024)(128)(2,1)S(1)}, bf16[1024]{0:T(1024)(128)(2,1)}, u32[]{:S(2)}) copy-start(bf16[1024]{0:T(1024)(128)(2,1)} %param.44) | copy-start | bytes 6148
  202.9 20.7 %copy-start.33 = (bf16[1024]{0:T(1024)(128)(2,1)S(1)}, bf16[1024]{0:T(1024)(128)(2,1)}, u32[]{:S(2)}) copy-start(bf16[1024]{0:T(1024)(128)(2,1)} %param.45) | copy-start | bytes 6148
  219.2 4.3 copy-start.18
  219.2 22.5 %all-to-all-start.1 = ((bf16[4,512,256]{1,2,0:T(8,128)(2,1)}), bf16[4,512,256]{1,2,0:T(8,128)(2,1)}, u32[]{:S(2)}, u32[]{:S(2)}) async-start(bf16[4,512,256]{1,2,0:T(8,128)(2,1)} %get-tuple-element.79), calls=%async_computation.1 | async-start | bytes 2097152 | tf_op jit(solution)/shard_map/all_to_all | solution.py:157
  223.4 310.5 %reduce-scatter.5.cloned.1.call-start = ((), (), s32[]{:S(2)}) async-start(), calls=%async_computation.14 | async-start | bytes 20971520 | tf_op jit(solution)/shard_map/reduce_scatter | solution.py:220
  284.5 10.3 %copy-start.8 = (bf16[512,1024]{1,0:T(8,128)(2,1)S(1)}, bf16[512,1024]{1,0:T(8,128)(2,1)}, u32[]{:S(2)}) copy-start(bf16[512,1024]{1,0:T(8,128)(2,1)} %param.28) | copy-start | bytes 3145732
  307.7 13.5 %copy-start.1 = (f32[512,1024]{1,0:T(8,128)S(1)}, f32[512,1024]{1,0:T(8,128)}, u32[]{:S(2)}) copy-start(f32[512,1024]{1,0:T(8,128)} %copy-done) | copy-start | bytes 6291460
  321.2 7.0 copy-start.39
  342.2 11.4 %copy-start.2 = (f32[512,1024]{1,0:T(8,128)S(1)}, f32[512,1024]{1,0:T(8,128)}, u32[]{:S(2)}) copy-start(f32[512,1024]{1,0:T(8,128)} %copy-done) | copy-start | bytes 6291460
  378.8 30.4 %all-to-all-start.2 = ((bf16[4,2,65536]{2,1,0:T(2,128)(2,1)}), bf16[4,2,65536]{2,1,0:T(2,128)(2,1)}, u32[]{:S(2)}, u32[]{:S(2)}) async-start(bf16[4,2,65536]{2,1,0:T(2,128)(2,1)} %reshape.269), calls=%async_computation.2 | async-start | bytes 2097152 | tf_op jit(solution)/shard_map/all_to_all | solution.py:191
  451.1 59.6 %all-to-all-start.3 = ((bf16[4,512,3,256]{1,3,2,0:T(8,128)(2,1)}), bf16[4,512,3,256]{1,3,2,0:T(8,128)(2,1)S(1)}, u32[]{:S(2)}, u32[]{:S(2)}) async-start(bf16[4,512,3,256]{1,3,2,0:T(8,128)(2,1)} %get-tuple-element.81), calls=%async_computation.3 | async-start | bytes 6291456 | tf_op jit(solution)/shard_map/all_to_all | solution.py:199
  454.9 164.4 %reduce-scatter.3.cloned.1.call-start = ((), (), s32[]{:S(2)}) async-start(), calls=%async_computation.13 | async-start | bytes 13107200 | tf_op jit(solution)/shard_map/reduce_scatter | solution.py:232
  510.9 9.1 copy-start.3
  533.9 473.0 %all-reduce.5.cloned.1.call-start = ((), (), s32[]{:S(2)}) async-start(), calls=%async_computation.15 | async-start | bytes 16777216 | tf_op jit(solution)/shard_map/psum | solution.py:238
  (22 other events, 62.4 us)
Sparse Core Ops, SparseCore 0:
  9.6 25.2 all-gather.7
  36.5 22.5 all-gather.11
  60.7 22.5 all-gather.9
  84.7 22.5 all-gather.13
  108.7 27.7 all-gather.15
  137.9 83.4 all-gather.17
  223.0 61.5 all-gather.19
  342.3 155.0 reduce-scatter.4
  534.0 85.2 reduce-scatter.2
  624.4 382.4 all-reduce.4
where the time goes:
time: 1030 us; the launch traced here: 1020 us
  waiting for transfers between devices  419 us (41%)
  blocking collectives  309 us (30%)
  matrix products  135 us (13%)
  local copies, waits for them, and re-layouts  75.6 us (7%)
  other arithmetic  52.9 us (5%)
  starting transfers between devices  17.8 us (2%)
  between operations  15.3 us (1%)
    psum x1, blocking collectives, local(): lax.psum((share_in, share_down, attn_share), 'dp')  268 us
    psum x1, waiting for transfers between devices, local(): lax.psum((share_in, share_down, attn_share), 'dp')  115 us
    all_to_all x1, waiting for transfers between devices, local(): lax.all_to_all(stacked, 'seq', split_axis=3, concat_axis=0, tiled=True)  77.5 us
    all_to_all x1, waiting for transfers between devices, local(): lax.all_to_all(grad_stack, 'seq', split_axis=0, concat_axis=3, tiled=True)  51.5 us
    psum x1, blocking collectives, local(): lax.psum((jnp.sum(grad_query_rows, axis=0, dtype=jnp.float32), jnp.sum(gr...  41.3 us
    unnamed x86, local copies, waits for them, and re-layouts  32.8 us
    reduce_scatter x1, waiting for transfers between devices, local(): lax.psum_scatter(jnp.concatenate([term_qkv, term_out, term_time], axis=1)...  29.4 us
    dot_general x1, matrix products, local(): jnp.einsum('td,fd->tf', first_low, full_in, preferred_element_type=jnp.fl...  27.2 us
  transfers between devices with their start and end apart: 14, of which 11 were waited for; matrix products, arithmetic and copies ran while one was open for 18% of the time, Pallas kernels for 0%

commit v1 on v0

--- a/solution.py
+++ b/solution.py
@@ -152,7 +152,10 @@
     stacked = jnp.stack([query_rows, key_rows, value_rows], axis=1).reshape(
         item_count, slot_count, 3, model_width
     )
-    head_side = lax.all_to_all(stacked, "seq", split_axis=3, concat_axis=0, tiled=True)
+    head_side = jnp.concatenate(
+        lax.all_to_all(jnp.stack(jnp.split(stacked, lax.axis_size("seq"), axis=3)), "seq", 0, 0),
+        axis=0,
+    )
     mixed_heads, log_totals = lax.map(attend_forward, (head_side, group_valid))
     mixed_rows = lax.all_to_all(
         mixed_heads, "seq", split_axis=0, concat_axis=2, tiled=True

time: 1030 us -> 1030 us (level)
    all_to_all x1, waiting for transfers between devices: 77.5 us -> 54.8 us  [local(): lax.all_to_all(jnp.stack(jnp.split(stacked, lax.axis_size('seq'), axis=3)...]
    all_gather x1, waiting for transfers between devices: 10.3 us -> 24.9 us  [local(): lax.all_gather(w_down, 'seq', axis=0, tiled=True)]
    unnamed x86 -> x84, local copies, waits for them, and re-layouts: 32.8 us -> 35.1 us
where the time goes in v1:
time: 1030 us; the launch traced here: 1020 us
  waiting for transfers between devices  415 us (40%)
  blocking collectives  309 us (30%)
  matrix products  134 us (13%)
  local copies, waits for them, and re-layouts  72.7 us (7%)
  other arithmetic  54.8 us (5%)
  starting transfers between devices  16.6 us (2%)
  between operations  15.3 us (1%)
    psum x1, blocking collectives, local(): lax.psum((share_in, share_down, attn_share), 'dp')  268 us
    psum x1, waiting for transfers between devices, local(): lax.psum((share_in, share_down, attn_share), 'dp')  115 us
    all_to_all x1, waiting for transfers between devices, local(): lax.all_to_all(jnp.stack(jnp.split(stacked, lax.axis_size('seq'), axis=3)...  54.8 us
    all_to_all x1, waiting for transfers between devices, local(): lax.all_to_all(grad_stack, 'seq', split_axis=0, concat_axis=3, tiled=True)  50.7 us
    psum x1, blocking collectives, local(): lax.psum((jnp.sum(grad_query_rows, axis=0, dtype=jnp.float32), jnp.sum(gr...  41.3 us
    unnamed x84, local copies, waits for them, and re-layouts  35.1 us
    reduce_scatter x1, waiting for transfers between devices, local(): lax.psum_scatter(jnp.concatenate([term_qkv, term_out, term_time], axis=1)...  29.4 us
    dot_general x1, matrix products, local(): jnp.einsum('td,fd->tf', first_low, full_in, preferred_element_type=jnp.fl...  27.7 us
  transfers between devices with their start and end apart: 14, of which 11 were waited for; matrix products, arithmetic and copies ran while one was open for 18% of the time, Pallas kernels for 0%

profile of v1, /device:TPU:0, one launch (start us, length us, event | category | flops | bytes accessed | tf_op | source)
XLA Modules:
  0.0 1017.9 jit_solution(3835326753239374456)
XLA Ops:
  11.2 23.7 %all-gather.8.cloned.1.call-done = bf16[1024,1024]{1,0:T(8,128)(2,1)} async-done(((bf16[256,1024]{1,0:T(8,128)(2,1)}), bf16[1024,1024]{1,0:T(8,128)(2,1)}) %all-gather.8.cloned.1.call-update) | async-done | bytes 2097168 | tf_op jit(solution)/shard_map/all_gather | solution.py:122
  36.9 22.2 %all-gather.12.cloned.1.call-done = bf16[1024,1024]{1,0:T(8,128)(2,1)} async-done(((bf16[256,1024]{1,0:T(8,128)(2,1)}), bf16[1024,1024]{1,0:T(8,128)(2,1)}) %all-gather.12.cloned.1.call-update) | async-done | bytes 2097168 | tf_op jit(solution)/shard_map/all_gather | solution.py:119
  61.9 21.3 %all-gather.10.cloned.1.call-done = bf16[1024,1024]{1,0:T(8,128)(2,1)} async-done(((bf16[256,1024]{1,0:T(8,128)(2,1)}), bf16[1024,1024]{1,0:T(8,128)(2,1)}) %all-gather.10.cloned.1.call-update) | async-done | bytes 2097168 | tf_op jit(solution)/shard_map/all_gather | solution.py:118
  86.1 21.2 %all-gather.14.cloned.1.call-done = bf16[1024,1024]{1,0:T(8,128)(2,1)} async-done(((bf16[256,1024]{1,0:T(8,128)(2,1)}), bf16[1024,1024]{1,0:T(8,128)(2,1)}) %all-gather.14.cloned.1.call-update) | async-done | bytes 2097168 | tf_op jit(solution)/shard_map/all_gather | solution.py:120
  117.4 54.8 %all-to-all-done = bf16[4,1,512,3,256]{4,2,3,1,0:T(8,128)(2,1)S(1)} async-done(((bf16[4,1,512,3,256]{4,2,3,1,0:T(8,128)(2,1)}), bf16[4,1,512,3,256]{4,2,3,1,0:T(8,128)(2,1)S(1)}, u32[]{:S(2)}, u32[]{:S(2)}) %all-to-all-start) | async-done | bytes 3145760 | tf_op jit(solution)/shard_map/all_to_all | solution.py:156
  177.1 16.3 %while.22 = (s32[]{:T(128)}, bf16[4,512,256]{1,2,0:T(8,128)(2,1)}, f32[4,4,512]{2,1,0:T(4,128)S(1)}, bf16[4,512,3,256]{1,3,2,0:T(8,128)(2,1)S(1)}, pred[4,512]{1,0:T(4,128)(4,1)S(1)}, /*index=5*/s32[]{:T(128)}) while((s32[]{:T(128)}, bf16[4,512,256]{1,2,0:T(8,128)(2,1)}, f32[4,4,512]{2,1,0:T(4,128)S(1)}, ...), condition=%wide.region_3.4_spmd, body=%wide.region_0.3_spmd.sunk | while | flops 281147392 | bytes 17370192 | solution.py:159
  193.4 4.3 all-to-all-start.1
  197.9 21.8 %all-to-all-done.1 = bf16[4,512,256]{1,2,0:T(8,128)(2,1)} async-done(((bf16[4,512,256]{1,2,0:T(8,128)(2,1)}), bf16[4,512,256]{1,2,0:T(8,128)(2,1)}, u32[]{:S(2)}, u32[]{:S(2)}) %all-to-all-start.1) | async-done | bytes 1048608 | tf_op jit(solution)/shard_map/all_to_all | solution.py:160
  225.0 27.7 %multiply_convert_fusion.1 = (bf16[512,4096]{1,0:T(8,128)(2,1)}, f32[512,4096]{1,0:T(8,128)}, f32[512,4096]{1,0:T(8,128)}) fusion(f32[4096]{0:T(1024)S(1)} %convert_element_type.170, bf16[4096,1024]{1,0:T(8,128)(2,1)} %all-gather.18.cloned.1.call-done, f32[512,1024]{1,0:T(8,128)} %copy-done, f32[1024]{0:T(1024)S(1)} %convert_element_type.168, ...), kind=kOutput, calls=%fused_computation.37 | convolution fusion | flops 4436000768 | bytes 31485952 | tf_op jit(solution)/shard_map/td,fd->tf/dot_general | solution.py:167
  252.7 24.9 %all-gather.20.cloned.1.call-done = bf16[4096,1024]{1,0:T(8,128)(2,1)} async-done(((bf16[1024,1024]{1,0:T(8,128)(2,1)}), bf16[4096,1024]{1,0:T(8,128)(2,1)}) %all-gather.20.cloned.1.call-update) | async-done | bytes 8388624 | tf_op jit(solution)/shard_map/all_gather | solution.py:124
  277.6 10.0 fusion.59
  293.6 7.1 convolution_convert_fusion
  300.7 13.5 %convert_reduce_fusion = (f32[4096]{0:T(1024)S(1)}, bf16[512,4096]{1,0:T(8,128)(2,1)S(1)}) fusion(f32[512,4096]{1,0:T(8,128)} %get-tuple-element.253, f32[512,4096]{1,0:T(8,128)} %get-tuple-element.282, f32[4096]{0:T(1024)S(1)} %convert_element_type.170, bf16[512,1024]{1,0:T(8,128)(2,1)S(1)} %get-tuple-element.243, ...), kind=kOutput, calls=%fused_computation.35 | convolution fusion | flops 4330614784 | bytes 30441472 | tf_op jit(solution)/shard_map/td,fd->tf/dot_general | solution.py:186
  314.3 7.0 convolution_convert_fusion.1
  321.3 13.9 %pad_maximum_fusion = bf16[4096,2048]{0,1:T(8,128)(2,1)} fusion(bf16[4096,1024]{0,1:T(8,128)(2,1)} %convolution_convert_fusion, bf16[4096,1024]{0,1:T(8,128)(2,1)} %convolution_convert_fusion.1), kind=kLoop, calls=%fused_computation.31 | loop fusion | flops 33554432 | bytes 33554432 | tf_op jit(solution)/shard_map/concatenate | solution.py:224
  335.3 11.4 %multiply_reduce_fusion.2 = (f32[1024]{0:T(1024)S(1)}, f32[512]{0:T(512)S(1)}, f32[1024]{0:T(1024)S(1)}, f32[512,1024]{1,0:T(8,128)S(1)}) fusion(f32[512,1024]{1,0:T(8,128)} %copy-done, f32[512]{0:T(512)S(1)} %fusion.42, f32[512]{0:T(512)S(1)} %broadcast_multiply_fusion.1, f32[1024]{0:T(1024)S(1)} %convert_element_type.167, ...), kind=kOutput, calls=%fused_computation.61 | convolution fusion | flops 4300207616 | bytes 18894848 | tf_op jit(solution)/shard_map/dot_general | solution.py:188
  352.9 6.2 copy.83
  359.6 9.0 reduce.7
  372.5 4.3 all-to-all-start.2
  376.8 26.1 %all-to-all-done.2 = bf16[4,2,65536]{2,1,0:T(2,128)(2,1)} async-done(((bf16[4,2,65536]{2,1,0:T(2,128)(2,1)}), bf16[4,2,65536]{2,1,0:T(2,128)(2,1)}, u32[]{:S(2)}, u32[]{:S(2)}) %all-to-all-start.2) | async-done | bytes 1048608 | tf_op jit(solution)/shard_map/all_to_all | solution.py:194
  409.7 35.0 %while.23 = (s32[]{:T(128)}, bf16[4,512,3,256]{1,3,2,0:T(8,128)(2,1)}, bf16[4,512,3,256]{1,3,2,0:T(8,128)(2,1)S(1)}, pred[4,512]{1,0:T(4,128)(4,1)S(1)}, f32[4,4...) while((s32[]{:T(128)}, bf16[4,512,3,256]{1,3,2,0:T(8,128)(2,1)}, ...), condition=%wide.region_14.15_spmd, body=%wide.region_12.14_spmd.sunk | while | flops 689829888 | bytes 39382108 | solution.py:201
  448.7 4.3 convolution_convert_fusion.3
  453.0 50.7 %all-to-all-done.3 = bf16[4,512,3,256]{1,3,2,0:T(8,128)(2,1)S(1)} async-done(((bf16[4,512,3,256]{1,3,2,0:T(8,128)(2,1)}), bf16[4,512,3,256]{1,3,2,0:T(8,128)(2,1)S(1)}, u32[]{:S(2)}, u32[]{:S(2)}) %all-to-all-start.3) | async-done | bytes 3145760 | tf_op jit(solution)/shard_map/all_to_all | solution.py:202
  517.0 9.9 pad_maximum_fusion.1
  527.0 6.8 fusion.55
  541.6 41.3 %all-reduce = (f32[1024]{0:T(1024)}, f32[1024]{0:T(1024)}, f32[1024]{0:T(1024)}, f32[1024]{0:T(1024)}, f32[4096]{0:T(1024)}, /*index=5*/f32[1024]{0:T(1024)}, f3...) all-reduce(f32[1024]{0:T(1024)S(1)} %get-tuple-element.288, ...), channel_id=1, replica_groups=mesh['dp'=8,'seq'=4] {'dp','seq'}, use_global_device_ids=true, to_apply=%region_22.23 | all-reduce | flops 13312 | bytes 104448 | tf_op jit(solution)/shard_map/psum | solution.py:253
  583.0 29.4 %reduce-scatter.3.cloned.1.call-done = bf16[256,5120]{1,0:T(8,128)(2,1)} async-done(((bf16[1024,5120]{1,0:T(8,128)(2,1)}), bf16[256,5120]{1,0:T(8,128)(2,1)}) %reduce-scatter.3.cloned.1.call-update) | async-done | bytes 2621456 | tf_op jit(solution)/shard_map/reduce_scatter | solution.py:235
  612.3 267.6 %all-reduce.6 = f32[256,5120]{1,0:T(8,128)} all-reduce(bf16[256,5120]{1,0:T(8,128)(2,1)} %reduce-scatter.3.cloned.1.call-done), channel_id=1, replica_groups=mesh['dp'=8,'seq'=4] {'dp'}, use_global_device_ids=true, to_apply=%region_17.18 | all-reduce | flops 1310720 | bytes 7864320 | tf_op jit(solution)/shard_map/psum | solution.py:241
  880.0 5.0 fusion.54
  885.0 114.9 %all-reduce.5.cloned.1.call-done = (f32[1024,1024]{0,1:T(8,128)}, f32[1024,1024]{0,1:T(8,128)}) async-done(((f32[1024,1024]{0,1:T(8,128)}, f32[1024,1024]{0,1:T(8,128)}), (f32[1024,1024]{0,1:T(8,128)}, f32[1024,1024]{0,1:T(8,128)})) %all-reduce.5.cloned.1.call-update) | async-done | bytes 8388624 | tf_op jit(solution)/shard_map/psum | solution.py:241
  999.9 5.3 copy.90
  1005.2 5.3 copy.91
  (241 shorter events, 131.4 us)
Async XLA Ops:
  7.2 27.7 %copy-start.21 = (bf16[1,1024]{1,0:T(2,128)(2,1)S(1)}, bf16[1,1024]{1,0:T(2,128)(2,1)}, u32[]{:S(2)}) copy-start(bf16[1,1024]{1,0:T(2,128)(2,1)} %param.26) | copy-start | bytes 6148
  7.2 27.7 %all-gather.8.cloned.1.call-start = ((), (), s32[]{:S(2)}) async-start(), calls=%async_computation.6 | async-start | bytes 2621440 | tf_op jit(solution)/shard_map/all_gather | solution.py:122
  8.0 28.9 %copy-start.26 = (bf16[1024]{0:T(1024)(128)(2,1)S(1)}, bf16[1024]{0:T(1024)(128)(2,1)}, u32[]{:S(2)}) copy-start(bf16[1024]{0:T(1024)(128)(2,1)} %param.39) | copy-start | bytes 6148
  8.0 51.1 %copy-start.13 = (bf16[512,1024]{1,0:T(8,128)(2,1)S(1)}, bf16[512,1024]{1,0:T(8,128)(2,1)}, u32[]{:S(2)}) copy-start(bf16[512,1024]{1,0:T(8,128)(2,1)} %param.25) | copy-start | bytes 3145732
  8.0 51.1 %all-gather.12.cloned.1.call-start = ((), (), s32[]{:S(2)}) async-start(), calls=%async_computation.8 | async-start | bytes 2621440 | tf_op jit(solution)/shard_map/all_gather | solution.py:119
  8.7 74.5 %all-gather.10.cloned.1.call-start = ((), (), s32[]{:S(2)}) async-start(), calls=%async_computation.7 | async-start | bytes 2621440 | tf_op jit(solution)/shard_map/all_gather | solution.py:118
  9.5 97.8 %all-gather.14.cloned.1.call-start = ((), (), s32[]{:S(2)}) async-start(), calls=%async_computation.9 | async-start | bytes 2621440 | tf_op jit(solution)/shard_map/all_gather | solution.py:120
  10.0 187.9 %all-gather.16.cloned.1.call-start = ((), (), s32[]{:S(2)}) async-start(), calls=%async_computation.10 | async-start | bytes 2621440 | tf_op jit(solution)/shard_map/all_gather | solution.py:121
  10.6 214.3 %all-gather.18.cloned.1.call-start = ((), (), s32[]{:S(2)}) async-start(), calls=%async_computation.11 | async-start | bytes 10485760 | tf_op jit(solution)/shard_map/all_gather | solution.py:123
  36.9 182.8 %copy-start.15 = (f32[1024]{0:T(1024)}, f32[1024]{0:T(1024)S(1)}, u32[]{:S(2)}) copy-start(f32[1024]{0:T(1024)S(1)} %convert_add_fusion.1) | copy-start | bytes 12292
  112.6 4.7 copy-start.36
  112.6 59.6 %all-to-all-start = ((bf16[4,1,512,3,256]{4,2,3,1,0:T(8,128)(2,1)}), bf16[4,1,512,3,256]{4,2,3,1,0:T(8,128)(2,1)S(1)}, u32[]{:S(2)}, u32[]{:S(2)}) async-start(bf16[4,1,512,3,256]{4,2,3,1,0:T(8,128)(2,1)} %pad_maximum_fusion.2), calls=%async_computation | async-start | bytes 6291456 | tf_op jit(solution)/shard_map/all_to_all | solution.py:156
  116.5 161.0 %all-gather.20.cloned.1.call-start = ((), (), s32[]{:S(2)}) async-start(), calls=%async_computation.12 | async-start | bytes 10485760 | tf_op jit(solution)/shard_map/all_gather | solution.py:124
  177.1 20.7 %copy-start.27 = (bf16[1024]{0:T(1024)(128)(2,1)S(1)}, bf16[1024]{0:T(1024)(128)(2,1)}, u32[]{:S(2)}) copy-start(bf16[1024]{0:T(1024)(128)(2,1)} %param.38) | copy-start | bytes 6148
  177.1 20.7 %copy-start.28 = (bf16[1024]{0:T(1024)(128)(2,1)S(1)}, bf16[1024]{0:T(1024)(128)(2,1)}, u32[]{:S(2)}) copy-start(bf16[1024]{0:T(1024)(128)(2,1)} %param.42) | copy-start | bytes 6148
  177.1 20.7 %copy-start.29 = (bf16[1024]{0:T(1024)(128)(2,1)S(1)}, bf16[1024]{0:T(1024)(128)(2,1)}, u32[]{:S(2)}) copy-start(bf16[1024]{0:T(1024)(128)(2,1)} %param.43) | copy-start | bytes 6148
  177.1 20.7 %copy-start.23 = (bf16[4096]{0:T(1024)(128)(2,1)S(1)}, bf16[4096]{0:T(1024)(128)(2,1)}, u32[]{:S(2)}) copy-start(bf16[4096]{0:T(1024)(128)(2,1)} %param.40) | copy-start | bytes 24580
  177.1 20.7 %copy-start.30 = (bf16[1024]{0:T(1024)(128)(2,1)S(1)}, bf16[1024]{0:T(1024)(128)(2,1)}, u32[]{:S(2)}) copy-start(bf16[1024]{0:T(1024)(128)(2,1)} %param.41) | copy-start | bytes 6148
  177.1 20.7 %copy-start.31 = (bf16[1024]{0:T(1024)(128)(2,1)S(1)}, bf16[1024]{0:T(1024)(128)(2,1)}, u32[]{:S(2)}) copy-start(bf16[1024]{0:T(1024)(128)(2,1)} %param.44) | copy-start | bytes 6148
  177.1 20.8 %copy-start.32 = (bf16[1024]{0:T(1024)(128)(2,1)S(1)}, bf16[1024]{0:T(1024)(128)(2,1)}, u32[]{:S(2)}) copy-start(bf16[1024]{0:T(1024)(128)(2,1)} %param.45) | copy-start | bytes 6148
  193.4 4.3 copy-start.17
  193.4 26.3 %all-to-all-start.1 = ((bf16[4,512,256]{1,2,0:T(8,128)(2,1)}), bf16[4,512,256]{1,2,0:T(8,128)(2,1)}, u32[]{:S(2)}, u32[]{:S(2)}) async-start(bf16[4,512,256]{1,2,0:T(8,128)(2,1)} %get-tuple-element.79), calls=%async_computation.1 | async-start | bytes 2097152 | tf_op jit(solution)/shard_map/all_to_all | solution.py:160
  197.7 329.3 %reduce-scatter.5.cloned.1.call-start = ((), (), s32[]{:S(2)}) async-start(), calls=%async_computation.14 | async-start | bytes 20971520 | tf_op jit(solution)/shard_map/reduce_scatter | solution.py:223
  277.6 10.3 %copy-start.9 = (bf16[512,1024]{1,0:T(8,128)(2,1)S(1)}, bf16[512,1024]{1,0:T(8,128)(2,1)}, u32[]{:S(2)}) copy-start(bf16[512,1024]{1,0:T(8,128)(2,1)} %param.28) | copy-start | bytes 3145732
  300.7 13.6 %copy-start.1 = (f32[512,1024]{1,0:T(8,128)S(1)}, f32[512,1024]{1,0:T(8,128)}, u32[]{:S(2)}) copy-start(f32[512,1024]{1,0:T(8,128)} %copy-done) | copy-start | bytes 6291460
  314.3 7.0 copy-start.38
  335.2 11.5 %copy-start.2 = (f32[512,1024]{1,0:T(8,128)S(1)}, f32[512,1024]{1,0:T(8,128)}, u32[]{:S(2)}) copy-start(f32[512,1024]{1,0:T(8,128)} %copy-done) | copy-start | bytes 6291460
  372.5 30.4 %all-to-all-start.2 = ((bf16[4,2,65536]{2,1,0:T(2,128)(2,1)}), bf16[4,2,65536]{2,1,0:T(2,128)(2,1)}, u32[]{:S(2)}, u32[]{:S(2)}) async-start(bf16[4,2,65536]{2,1,0:T(2,128)(2,1)} %reshape.273), calls=%async_computation.2 | async-start | bytes 2097152 | tf_op jit(solution)/shard_map/all_to_all | solution.py:194
  444.8 58.9 %all-to-all-start.3 = ((bf16[4,512,3,256]{1,3,2,0:T(8,128)(2,1)}), bf16[4,512,3,256]{1,3,2,0:T(8,128)(2,1)S(1)}, u32[]{:S(2)}, u32[]{:S(2)}) async-start(bf16[4,512,3,256]{1,3,2,0:T(8,128)(2,1)} %get-tuple-element.81), calls=%async_computation.3 | async-start | bytes 6291456 | tf_op jit(solution)/shard_map/all_to_all | solution.py:202
  448.6 163.7 %reduce-scatter.3.cloned.1.call-start = ((), (), s32[]{:S(2)}) async-start(), calls=%async_computation.13 | async-start | bytes 13107200 | tf_op jit(solution)/shard_map/reduce_scatter | solution.py:235
  503.9 9.1 copy-start.4
  526.9 473.0 %all-reduce.5.cloned.1.call-start = ((), (), s32[]{:S(2)}) async-start(), calls=%async_computation.15 | async-start | bytes 16777216 | tf_op jit(solution)/shard_map/psum | solution.py:241
  (21 other events, 57.9 us)
Sparse Core Ops, SparseCore 0:
  9.6 25.2 all-gather.7
  36.5 22.5 all-gather.11
  60.6 22.5 all-gather.9
  84.6 22.5 all-gather.13
  108.6 32.7 all-gather.15
  142.9 74.5 all-gather.17
  219.0 58.5 all-gather.19
  335.4 154.3 reduce-scatter.4
  527.0 85.2 reduce-scatter.2
  617.4 382.4 all-reduce.4
